TPU v7x, 256 devices: a whole 4x4x8 slice. The times are simulated.
256 devices in a mesh: dp: 2 (over y_hi), seq: 128 (over y_lo, z, x, core).
Axes of the slice: x: 4, y: 4 (y_hi: 2, y_lo: 2; y = y_hi * 2 + y_lo), z: 8, core: 2. Of those that a mesh axis runs over, the one named last changes fastest.
Arguments:
- values: bfloat16 [2, 32768, 256], P('dp', 'seq'), may hold values from -6 to 6
- gate_acts: bfloat16 [2, 32768, 256], P('dp', 'seq'), may hold values from -6 to 6
- filter_taps: bfloat16 [32768, 256], P('seq'), may hold values from -1.4 to 1.4
- skip_bias: float32 [256], replicated, may hold values from 0.25 to 1.75
- grad_out: bfloat16 [2, 32768, 256], P('dp', 'seq'), may hold values from -6 to 6
Outputs:
- mixed_out: bfloat16 [2, 32768, 256], P('dp', 'seq')
- grad_values: bfloat16 [2, 32768, 256], P('dp', 'seq')
- grad_gates: bfloat16 [2, 32768, 256], P('dp', 'seq')
- grad_filter: float32 [32768, 256], P('seq', 'dp')
All inputs are finite; a program needn't handle non-finite values.
Results may differ from a plain program's by a relative error of at most 0.007.
Values may be sent and summed in bfloat16 or wider, within the bound.
A program may use at most 64 MiB of HBM per device.

v0:
```python
import math

import jax
import jax.numpy as jnp
from jax import lax
from jax.sharding import PartitionSpec as P

ALL = ("dp", "seq")

precise = lax.Precision.HIGH


def contract(pattern, left, right):
    return jnp.einsum(
        pattern, left, right, precision=precise, preferred_element_type=jnp.float32
    )


def angles(first_idx, second_idx, period):
    turns = first_idx[:, None] * second_idx[None, :] % period
    phase = turns.astype(jnp.float32) * (2.0 * math.pi / period)
    return (jnp.cos(phase), jnp.sin(phase))


def spectra(x_re, x_im, outer, inner):
    half = outer // 2
    padded = outer * inner
    k_idx = jnp.arange(outer, dtype=jnp.int32)
    a_idx = jnp.arange(half, dtype=jnp.int32)
    b_idx = jnp.arange(inner, dtype=jnp.int32)
    cos1, sin1 = angles(k_idx, a_idx, outer)
    y_re = contract("ka,xab->xkb", cos1, x_re) + contract("ka,xab->xkb", sin1, x_im)
    y_im = contract("ka,xab->xkb", cos1, x_im) - contract("ka,xab->xkb", sin1, x_re)
    tw_re, tw_im = angles(k_idx, b_idx, padded)
    y_re, y_im = (y_re * tw_re + y_im * tw_im, y_im * tw_re - y_re * tw_im)
    cos2, sin2 = angles(b_idx, b_idx, inner)
    z_re = contract("xkb,bl->xkl", y_re, cos2) + contract("xkb,bl->xkl", y_im, sin2)
    z_im = contract("xkb,bl->xkl", y_im, cos2) - contract("xkb,bl->xkl", y_re, sin2)
    return z_re, z_im


def timeline(z_re, z_im, outer, inner):
    half = outer // 2
    padded = outer * inner
    k_idx = jnp.arange(outer, dtype=jnp.int32)
    a_idx = jnp.arange(half, dtype=jnp.int32)
    b_idx = jnp.arange(inner, dtype=jnp.int32)
    cos2, sin2 = angles(b_idx, b_idx, inner)
    u_re = contract("xkl,lb->xkb", z_re, cos2) - contract("xkl,lb->xkb", z_im, sin2)
    u_im = contract("xkl,lb->xkb", z_im, cos2) + contract("xkl,lb->xkb", z_re, sin2)
    tw_re, tw_im = angles(k_idx, b_idx, padded)
    u_re, u_im = (u_re * tw_re - u_im * tw_im, u_im * tw_re + u_re * tw_im)
    cos1, sin1 = angles(a_idx, k_idx, outer)
    s_re = contract("ak,xkb->xab", cos1, u_re) - contract("ak,xkb->xab", sin1, u_im)
    s_im = contract("ak,xkb->xab", cos1, u_im) + contract("ak,xkb->xab", sin1, u_re)
    return s_re * (1.0 / padded), s_im * (1.0 / padded)


def on_device(values, gate_acts, filter_taps, skip_bias, grad_out):
    dp_count = lax.axis_size("dp")
    seq_count = lax.axis_size("seq")
    dev_count = dp_count * seq_count
    dp_index = lax.axis_index("dp")
    me = dp_index * seq_count + lax.axis_index("seq")
    rows = values.shape[1]
    channels = values.shape[2]
    per = channels // dev_count
    tap_rows = rows // dp_count

    taps_part = lax.dynamic_slice_in_dim(filter_taps, dp_index * tap_rows, tap_rows, 0)
    send = jnp.concatenate(
        [values[0].T, gate_acts[0].T, grad_out[0].T, taps_part.T], axis=1
    ).reshape(dev_count, per, 3 * rows + tap_rows)
    got = lax.all_to_all(send, ALL, 0, 0, tiled=True)

    def owned(lo, width):
        part = got[:, :, lo : lo + width].reshape(dp_count, seq_count, per, width)
        return part.transpose(2, 0, 1, 3)

    val = owned(0, rows)
    gate = owned(rows, rows)
    cot = owned(2 * rows, rows)
    taps = owned(3 * rows, tap_rows).transpose(0, 2, 1, 3).reshape(per, 1, seq_count, rows)
    grad_sig = (cot.astype(jnp.float32) * gate.astype(jnp.float32)).astype(jnp.bfloat16)

    outer = 2 * seq_count
    sig_re = jnp.stack([val[:, 0], grad_sig[:, 0], taps[:, 0]], axis=1).astype(jnp.float32)
    sig_im = jnp.stack(
        [val[:, 1], grad_sig[:, 1], jnp.zeros_like(taps[:, 0])], axis=1
    ).astype(jnp.float32)
    z_re, z_im = spectra(
        sig_re.reshape(per * 3, seq_count, rows), sig_im.reshape(per * 3, seq_count, rows), outer, rows
    )
    z_re = z_re.reshape(per, 3, outer, rows)
    z_im = z_im.reshape(per, 3, outer, rows)
    v_re, v_im = z_re[:, 0], z_im[:, 0]
    g_re, g_im = z_re[:, 1], z_im[:, 1]
    t_re, t_im = z_re[:, 2], z_im[:, 2]
    conv_re = v_re * t_re - v_im * t_im
    conv_im = v_re * t_im + v_im * t_re
    corr_re = g_re * t_re + g_im * t_im
    corr_im = g_im * t_re - g_re * t_im
    filt_re = v_re * g_re + v_im * g_im
    filt_im = v_re * g_im - v_im * g_re
    prod_re = jnp.stack([conv_re, corr_re, filt_re], axis=1).reshape(per * 3, outer, rows)
    prod_im = jnp.stack([conv_im, corr_im, filt_im], axis=1).reshape(per * 3, outer, rows)
    out_re, out_im = timeline(prod_re, prod_im, outer, rows)
    out_re = out_re.reshape(per, 3, seq_count, rows)
    out_im = out_im.reshape(per, 3, seq_count, rows)
    conv_part = jnp.stack([out_re[:, 0], out_im[:, 0]], axis=1)
    back_part = jnp.stack([out_re[:, 1], out_im[:, 1]], axis=1)
    total = dp_count * seq_count * rows
    grad_filter = out_re[:, 2] * (1.0 / math.sqrt(total))

    bias = lax.dynamic_slice_in_dim(skip_bias, me * per, per, 0)[:, None, None, None]
    hyena_pre = conv_part + bias * val.astype(jnp.float32)
    mixed_out = (gate.astype(jnp.float32) * hyena_pre).astype(jnp.bfloat16)
    grad_gates = (cot.astype(jnp.float32) * hyena_pre).astype(jnp.bfloat16)
    grad_values = (back_part + bias * grad_sig.astype(jnp.float32)).astype(jnp.bfloat16)

    back = jnp.concatenate([mixed_out, grad_values, grad_gates], axis=3)
    back = back.transpose(1, 2, 0, 3).reshape(dev_count, per, 3 * rows)
    back = lax.all_to_all(back, ALL, 0, 0, tiled=True).reshape(channels, 3, rows)
    mixed_out = back[:, 0].T[None]
    grad_values = back[:, 1].T[None]
    grad_gates = back[:, 2].T[None]

    filt = lax.all_to_all(grad_filter.transpose(1, 0, 2), "seq", 0, 0, tiled=True)
    grad_filter = filt.reshape(seq_count * per, rows).T
    return (mixed_out, grad_values, grad_gates, grad_filter)


def solution(mesh):
    in_specs = (P("dp", "seq", None), P("dp", "seq", None), P("seq", None), P(), P("dp", "seq", None))
    out_specs = (P("dp", "seq", None), P("dp", "seq", None), P("dp", "seq", None), P("seq", "dp"))
    return jax.shard_map(
        on_device, mesh=mesh, in_specs=in_specs, out_specs=out_specs, check_vma=False
    )
```

profile of v0, /device:TPU:1, one launch (start us, length us, event | category | flops | bytes accessed | tf_op | source)
XLA Modules:
  0.0 111.9 jit_solution(11626701776308978767)
XLA Ops:
  0.7 0.9 copy-done
  2.6 0.8 copy-done.2
  4.9 0.9 reduce
  5.9 1.2 %reshape.259 = bf16[256,2,448]{2,1,0:T(2,128)(2,1)} reshape(bf16[256,896]{1,0:T(8,128)(2,1)S(1)} %reduce) | data formatting | bytes 917504
  7.1 15.6 %all-to-all-start = ((bf16[256,2,448]{2,1,0:T(2,128)(2,1)}), bf16[256,2,448]{2,1,0:T(2,128)(2,1)S(1)}, u32[]{:S(2)}, u32[]{:S(2)}) async-start(bf16[256,2,448]{2,1,0:T(2,128)(2,1)} %reshape.259), calls=%async_computation | async-start | bytes 1048576 | tf_op jit(solution)/shard_map/all_to_all | solution.py:74
  22.8 1.0 fusion.67
  23.9 1.0 fusion.66
  26.3 16.9 %all-to-all-done = bf16[256,2,448]{2,1,0:T(2,128)(2,1)S(1)} async-done(((bf16[256,2,448]{2,1,0:T(2,128)(2,1)}), bf16[256,2,448]{2,1,0:T(2,128)(2,1)S(1)}, u32[]{:S(2)}, u32[]{:S(2)}) %all-to-all-start) | async-done | bytes 458784 | tf_op jit(solution)/shard_map/all_to_all | solution.py:74
  43.2 1.1 %reshape.260 = bf16[256,1,896]{2,1,0:T(2,128)(2,1)S(1)} reshape(bf16[256,2,448]{2,1,0:T(2,128)(2,1)S(1)} %all-to-all-done) | data formatting | bytes 917504
  44.5 0.8 fusion.158
  46.1 0.9 fusion.52
  46.9 0.9 fusion.35
  47.8 0.9 fusion.3
  48.7 0.9 fusion.2
  49.5 1.7 %fusion.24 = f32[3,256,256]{2,1,0:T(8,128)S(1)} fusion(f32[3,256,256]{1,2,0:T(8,128)S(1)} %fusion.3, f32[3,256,256]{1,2,0:T(8,128)S(1)} %fusion.2, f32[256,256]{0,1:T(8,128)S(1)} %copy.124, f32[256,256]{0,1:T(8,128)S(1)} %copy.123), kind=kOutput, calls=%fused_computation.52 | convolution fusion | flops 303497216 | bytes 2883584 | tf_op jit(solution)/shard_map/xkb,bl->xkl/dot_general | solution.py:14
  51.3 1.7 %fusion.26 = f32[3,256,256]{2,1,0:T(8,128)S(1)} fusion(f32[3,256,256]{1,2,0:T(8,128)S(1)} %fusion.2, f32[3,256,256]{1,2,0:T(8,128)S(1)} %fusion.3, f32[256,256]{0,1:T(8,128)S(1)} %copy.124, f32[256,256]{0,1:T(8,128)S(1)} %copy.123), kind=kOutput, calls=%fused_computation.54 | convolution fusion | flops 303497216 | bytes 2883584 | tf_op jit(solution)/shard_map/xkb,bl->xkl/dot_general | solution.py:14
  53.0 1.7 %fusion = f32[1,3,256,256]{3,2,1,0:T(8,128)S(1)} fusion(f32[3,256,256]{2,1,0:T(8,128)S(1)} %fusion.24, f32[3,256,256]{1,2,0:T(8,128)S(1)} %fusion.2, f32[3,256,256]{1,2,0:T(8,128)S(1)} %fusion.3, f32[256,256]{0,1:T(8,128)S(1)} %copy.124, f32[256,256]{0,1:T(8,128)S(1)} %copy.123), kind=kOutput, calls=%fused_computation.3 | convolution fusion | flops 303693824 | bytes 3670016 | tf_op jit(solution)/shard_map/xkb,bl->xkl/dot_general | solution.py:14
  54.7 1.7 %fusion.1 = f32[1,3,256,256]{3,2,1,0:T(8,128)S(1)} fusion(f32[3,256,256]{2,1,0:T(8,128)S(1)} %fusion.26, f32[3,256,256]{1,2,0:T(8,128)S(1)} %fusion.3, f32[3,256,256]{1,2,0:T(8,128)S(1)} %fusion.2, f32[256,256]{0,1:T(8,128)S(1)} %copy.124, f32[256,256]{0,1:T(8,128)S(1)} %copy.123), kind=kOutput, calls=%fused_computation.5 | convolution fusion | flops 303693824 | bytes 3670016 | tf_op jit(solution)/shard_map/xkb,bl->xkl/dot_general | solution.py:14
  56.9 1.5 %fusion.9 = f32[3,256,256]{1,2,0:T(8,128)S(1)} fusion(f32[1,1,256,256]{3,2,1,0:T(8,128)S(1)} %get-tuple-element.25, f32[1,1,256,256]{3,2,1,0:T(8,128)S(1)} %get-tuple-element.29, f32[1,1,256,256]{3,2,1,0:T(8,128)S(1)} %get-tuple-element.28), kind=kOutput, calls=%fused_computation.23 | convolution fusion | flops 303300608 | bytes 1572864 | tf_op jit(solution)/shard_map/xkl,lb->xkb/dot_general | solution.py:14
  58.4 1.5 %fusion.8 = f32[3,256,256]{1,2,0:T(8,128)S(1)} fusion(f32[1,1,256,256]{3,2,1,0:T(8,128)S(1)} %get-tuple-element.27, f32[1,1,256,256]{3,2,1,0:T(8,128)S(1)} %get-tuple-element.26, f32[1,1,256,256]{3,2,1,0:T(8,128)S(1)} %get-tuple-element.24), kind=kOutput, calls=%fused_computation.22 | convolution fusion | flops 303300608 | bytes 1572864 | tf_op jit(solution)/shard_map/xkl,lb->xkb/dot_general | solution.py:14
  59.9 1.5 %convolution_subtract_fusion = f32[3,256,256]{1,2,0:T(8,128)S(1)} fusion(f32[3,256,256]{1,2,0:T(8,128)S(1)} %fusion.9, f32[1,1,256,256]{3,2,1,0:T(8,128)S(1)} %get-tuple-element.27, f32[1,1,256,256]{3,2,1,0:T(8,128)S(1)} %get-tuple-element.26, f32[1,1,256,256]{3,2,1,0:T(8,128)S(1)} %get-tuple-element.24), kind=kOutput, calls=%fused_computation.1 | convolution fusion | flops 303497216 | bytes 2359296 | tf_op jit(solution)/shard_map/xkl,lb->xkb/dot_general | solution.py:14
  61.4 1.5 %convolution_add_fusion = f32[3,256,256]{1,2,0:T(8,128)S(1)} fusion(f32[3,256,256]{1,2,0:T(8,128)S(1)} %fusion.8, f32[1,1,256,256]{3,2,1,0:T(8,128)S(1)} %get-tuple-element.25, f32[1,1,256,256]{3,2,1,0:T(8,128)S(1)} %get-tuple-element.29, f32[1,1,256,256]{3,2,1,0:T(8,128)S(1)} %get-tuple-element.28), kind=kOutput, calls=%fused_computation | convolution fusion | flops 303497216 | bytes 2359296 | tf_op jit(solution)/shard_map/xkl,lb->xkb/dot_general | solution.py:14
  62.9 1.1 fusion.45
  64.0 1.1 fusion.47
  65.1 1.1 fusion.5
  66.2 1.1 fusion.7
  68.1 6.0 %all-to-all-start.2 = ((f32[128,1,256]{2,1,0:T(1,128)}), f32[128,1,256]{2,1,0:T(1,128)S(1)}, u32[]{:S(2)}, u32[]{:S(2)}) async-start(f32[128,1,256]{2,1,0:T(1,128)} %copy.139), calls=%async_computation.2 | async-start | bytes 262144 | tf_op jit(solution)/shard_map/all_to_all | solution.py:128
  75.5 0.9 reduce.1
  76.4 0.8 reshape.261
  77.3 9.1 %all-to-all-done.2 = f32[128,1,256]{2,1,0:T(1,128)S(1)} async-done(((f32[128,1,256]{2,1,0:T(1,128)}), f32[128,1,256]{2,1,0:T(1,128)S(1)}, u32[]{:S(2)}, u32[]{:S(2)}) %all-to-all-start.2) | async-done | bytes 131104 | tf_op jit(solution)/shard_map/all_to_all | solution.py:128
  86.4 5.4 %all-to-all-start.1 = ((bf16[256,2,384]{2,1,0:T(2,128)(2,1)}), bf16[256,2,384]{2,1,0:T(2,128)(2,1)S(1)}, u32[]{:S(2)}, u32[]{:S(2)}) async-start(bf16[256,2,384]{2,1,0:T(2,128)(2,1)} %reshape.261), calls=%async_computation.1 | async-start | bytes 786432 | tf_op jit(solution)/shard_map/all_to_all | solution.py:123
  92.6 17.5 %all-to-all-done.1 = bf16[256,2,384]{2,1,0:T(2,128)(2,1)S(1)} async-done(((bf16[256,2,384]{2,1,0:T(2,128)(2,1)}), bf16[256,2,384]{2,1,0:T(2,128)(2,1)S(1)}, u32[]{:S(2)}, u32[]{:S(2)}) %all-to-all-start.1) | async-done | bytes 393248 | tf_op jit(solution)/shard_map/all_to_all | solution.py:123
  (43 shorter events, 10.2 us)
Async XLA Ops:
  0.6 0.9 copy-start
  1.5 0.9 copy-start.1
  2.4 0.9 copy-start.2
  3.4 0.9 copy-start.3
  7.1 36.1 %all-to-all-start = ((bf16[256,2,448]{2,1,0:T(2,128)(2,1)}), bf16[256,2,448]{2,1,0:T(2,128)(2,1)S(1)}, u32[]{:S(2)}, u32[]{:S(2)}) async-start(bf16[256,2,448]{2,1,0:T(2,128)(2,1)} %reshape.259), calls=%async_computation | async-start | bytes 1048576 | tf_op jit(solution)/shard_map/all_to_all | solution.py:74
  25.0 0.7 copy-start.4
  68.1 18.4 %all-to-all-start.2 = ((f32[128,1,256]{2,1,0:T(1,128)}), f32[128,1,256]{2,1,0:T(1,128)S(1)}, u32[]{:S(2)}, u32[]{:S(2)}) async-start(f32[128,1,256]{2,1,0:T(1,128)} %copy.139), calls=%async_computation.2 | async-start | bytes 262144 | tf_op jit(solution)/shard_map/all_to_all | solution.py:128
  86.4 23.7 %all-to-all-start.1 = ((bf16[256,2,384]{2,1,0:T(2,128)(2,1)}), bf16[256,2,384]{2,1,0:T(2,128)(2,1)S(1)}, u32[]{:S(2)}, u32[]{:S(2)}) async-start(bf16[256,2,384]{2,1,0:T(2,128)(2,1)} %reshape.261), calls=%async_computation.1 | async-start | bytes 786432 | tf_op jit(solution)/shard_map/all_to_all | solution.py:123
where the time goes:
time: 112 us
  waiting for transfers between devices  43.6 us (39%)
  starting transfers between devices  27 us (24%)
  matrix products  20.6 us (18%)
  local copies, waits for them, and re-layouts  13.9 us (12%)
  other arithmetic  5.81 us (5%)
    dot_general x16, matrix products, contract(): jnp.einsum(pattern, left, right, precision=precise, preferred_element_typ...  20.6 us
    all_to_all x1, waiting for transfers between devices, on_device(): lax.all_to_all(back, ALL, 0, 0, tiled=True).reshape(channels, 3, rows)  17.5 us
    all_to_all x1, waiting for transfers between devices, on_device(): got = lax.all_to_all(send, ALL, 0, 0, tiled=True)  16.9 us
    all_to_all x1, starting transfers between devices, on_device(): got = lax.all_to_all(send, ALL, 0, 0, tiled=True)  15.6 us
    all_to_all x1, waiting for transfers between devices, on_device(): lax.all_to_all(grad_filter.transpose(1, 0, 2), 'seq', 0, 0, tiled=True)  9.14 us
    unnamed x24, local copies, waits for them, and re-layouts  8.35 us
    all_to_all x1, starting transfers between devices, on_device(): lax.all_to_all(grad_filter.transpose(1, 0, 2), 'seq', 0, 0, tiled=True)  5.95 us
    all_to_all x1, starting transfers between devices, on_device(): lax.all_to_all(back, ALL, 0, 0, tiled=True).reshape(channels, 3, rows)  5.41 us
  transfers between devices with their start and end apart: 3, of which 3 were waited for; matrix products, arithmetic and copies ran while one was open for 6% of the time, Pallas kernels for 0%

commit v1 on v0

--- a/solution.py
+++ b/solution.py
@@ -68,9 +68,12 @@
     tap_rows = rows // dp_count
 
     taps_part = lax.dynamic_slice_in_dim(filter_taps, dp_index * tap_rows, tap_rows, 0)
-    send = jnp.concatenate(
-        [values[0].T, gate_acts[0].T, grad_out[0].T, taps_part.T], axis=1
-    ).reshape(dev_count, per, 3 * rows + tap_rows)
+    gate_grad = (grad_out[0].astype(jnp.float32) * gate_acts[0].astype(jnp.float32)).astype(
+        jnp.bfloat16
+    )
+    send = jnp.concatenate([values[0].T, gate_grad.T, taps_part.T], axis=1).reshape(
+        dev_count, per, 2 * rows + tap_rows
+    )
     got = lax.all_to_all(send, ALL, 0, 0, tiled=True)
 
     def owned(lo, width):
@@ -78,10 +81,8 @@
         return part.transpose(2, 0, 1, 3)
 
     val = owned(0, rows)
-    gate = owned(rows, rows)
-    cot = owned(2 * rows, rows)
-    taps = owned(3 * rows, tap_rows).transpose(0, 2, 1, 3).reshape(per, 1, seq_count, rows)
-    grad_sig = (cot.astype(jnp.float32) * gate.astype(jnp.float32)).astype(jnp.bfloat16)
+    grad_sig = owned(rows, rows)
+    taps = owned(2 * rows, tap_rows).transpose(0, 2, 1, 3).reshape(per, 1, seq_count, rows)
 
     outer = 2 * seq_count
     sig_re = jnp.stack([val[:, 0], grad_sig[:, 0], taps[:, 0]], axis=1).astype(jnp.float32)
@@ -110,23 +111,23 @@
     conv_part = jnp.stack([out_re[:, 0], out_im[:, 0]], axis=1)
     back_part = jnp.stack([out_re[:, 1], out_im[:, 1]], axis=1)
     total = dp_count * seq_count * rows
-    grad_filter = out_re[:, 2] * (1.0 / math.sqrt(total))
+    grad_filter = (out_re[:, 2] * (1.0 / math.sqrt(total))).astype(jnp.bfloat16)
 
     bias = lax.dynamic_slice_in_dim(skip_bias, me * per, per, 0)[:, None, None, None]
-    hyena_pre = conv_part + bias * val.astype(jnp.float32)
-    mixed_out = (gate.astype(jnp.float32) * hyena_pre).astype(jnp.bfloat16)
-    grad_gates = (cot.astype(jnp.float32) * hyena_pre).astype(jnp.bfloat16)
+    hyena_pre = (conv_part + bias * val.astype(jnp.float32)).astype(jnp.bfloat16)
     grad_values = (back_part + bias * grad_sig.astype(jnp.float32)).astype(jnp.bfloat16)
 
-    back = jnp.concatenate([mixed_out, grad_values, grad_gates], axis=3)
+    filt_rep = jnp.broadcast_to(grad_filter[:, None], (per, dp_count, seq_count, rows))
+    back = jnp.concatenate([hyena_pre, grad_values, filt_rep], axis=3)
     back = back.transpose(1, 2, 0, 3).reshape(dev_count, per, 3 * rows)
     back = lax.all_to_all(back, ALL, 0, 0, tiled=True).reshape(channels, 3, rows)
-    mixed_out = back[:, 0].T[None]
+    hyena_pre = back[:, 0].T.astype(jnp.float32)
     grad_values = back[:, 1].T[None]
-    grad_gates = back[:, 2].T[None]
-
-    filt = lax.all_to_all(grad_filter.transpose(1, 0, 2), "seq", 0, 0, tiled=True)
-    grad_filter = filt.reshape(seq_count * per, rows).T
+    share = channels // dp_count
+    grad_filter = lax.dynamic_slice_in_dim(back[:, 2], dp_index * share, share, 0)
+    grad_filter = grad_filter.T.astype(jnp.float32)
+    mixed_out = (gate_acts[0].astype(jnp.float32) * hyena_pre).astype(jnp.bfloat16)[None]
+    grad_gates = (grad_out[0].astype(jnp.float32) * hyena_pre).astype(jnp.bfloat16)[None]
     return (mixed_out, grad_values, grad_gates, grad_filter)
 
 

time: 112 us -> 91.7 us (0.82)
  waiting for transfers between devices: 43.6 us -> 14.6 us
  blocking collectives: 0 us -> 23.2 us
  starting transfers between devices: 27 us -> 15.6 us
  local copies, waits for them, and re-layouts: 13.9 us -> 8.42 us
  other arithmetic: 5.81 us -> 7.81 us
    all_to_all x2 -> x0, waiting for transfers between devices: 26.6 us -> none  [the longest x1 17.5 us: on_device(): lax.all_to_all(back, ALL, 0, 0, tiled=True).reshape(channels, 3, rows)]
    all_to_all x0 -> x1, blocking collectives: none -> 23.2 us  [on_device(): lax.all_to_all(back, ALL, 0, 0, tiled=True).reshape(channels, 3, rows)]
    all_to_all x2 -> x0, starting transfers between devices: 11.4 us -> none  [the longest x1 5.95 us: on_device(): lax.all_to_all(grad_filter.transpose(1, 0, 2), 'seq', 0, 0, tiled=True)]
    unnamed x24 -> x22, local copies, waits for them, and re-layouts: 8.35 us -> 4.77 us
    all_to_all x1, waiting for transfers between devices: 16.9 us -> 14.6 us  [on_device(): got = lax.all_to_all(send, ALL, 0, 0, tiled=True)]
  transfers between devices with their start and end apart: 3 -> 1, of which waited for: 3 -> 1; matrix products, arithmetic and copies ran while one was open for 6% -> 3% of each run, Pallas kernels for 0% -> 0%
where the time goes in v1:
time: 91.7 us; the launch traced here: 91.4 us
  blocking collectives  23.2 us (25%)
  matrix products  20.8 us (23%)
  starting transfers between devices  15.6 us (17%)
  waiting for transfers between devices  14.6 us (16%)
  local copies, waits for them, and re-layouts  8.42 us (9%)
  other arithmetic  7.81 us (9%)
  between operations  1.03 us (1%)
    all_to_all x1, blocking collectives, on_device(): lax.all_to_all(back, ALL, 0, 0, tiled=True).reshape(channels, 3, rows)  23.2 us
    dot_general x16, matrix products, contract(): jnp.einsum(pattern, left, right, precision=precise, preferred_element_typ...  20.8 us
    all_to_all x1, starting transfers between devices, on_device(): got = lax.all_to_all(send, ALL, 0, 0, tiled=True)  15.6 us
    all_to_all x1, waiting for transfers between devices, on_device(): got = lax.all_to_all(send, ALL, 0, 0, tiled=True)  14.6 us
    unnamed x22, local copies, waits for them, and re-layouts  4.77 us
  transfers between devices with their start and end apart: 1, of which 1 were waited for; matrix products, arithmetic and copies ran while one was open for 3% of the time, Pallas kernels for 0%

profile of v1, /device:TPU:1, one launch (start us, length us, event | category | flops | bytes accessed | tf_op | source)
XLA Modules:
  0.0 91.4 jit_solution(805582564582083058)
XLA Ops:
  0.7 0.9 copy-done
  1.6 1.0 %fusion.44 = bf16[256,256]{0,1:T(8,128)(2,1)S(1)} fusion(bf16[1,256,256]{2,1,0:T(8,128)(2,1)S(1)} %copy-done.1, bf16[1,256,256]{2,1,0:T(8,128)(2,1)} %param.6), kind=kLoop, calls=%fused_computation.88 | loop fusion | flops 262144 | bytes 393216 | tf_op jit(solution)/shard_map/transpose | solution.py:74
  3.1 0.9 reduce
  4.2 1.1 %reshape.215 = bf16[256,2,320]{2,1,0:T(2,128)(2,1)} reshape(bf16[256,640]{1,0:T(8,128)(2,1)S(1)} %copy.152) | data formatting | bytes 655360
  5.3 15.6 %all-to-all-start = ((bf16[256,2,320]{2,1,0:T(2,128)(2,1)}), bf16[256,2,320]{2,1,0:T(2,128)(2,1)S(1)}, u32[]{:S(2)}, u32[]{:S(2)}) async-start(bf16[256,2,320]{2,1,0:T(2,128)(2,1)} %reshape.215), calls=%async_computation | async-start | bytes 786432 | tf_op jit(solution)/shard_map/all_to_all | solution.py:77
  21.0 1.0 %fusion.71 = f32[256,256]{1,0:T(8,128)S(1)} fusion(), kind=kLoop, calls=%fused_computation.111 | loop fusion | flops 917504 | bytes 262144 | tf_op jit(solution)/shard_map/cos | solution.py:22
  22.1 1.0 %fusion.70 = f32[256,256]{1,0:T(8,128)S(1)} fusion(), kind=kLoop, calls=%fused_computation.110 | loop fusion | flops 917504 | bytes 262144 | tf_op jit(solution)/shard_map/sin | solution.py:22
  24.5 14.6 %all-to-all-done = bf16[256,2,320]{2,1,0:T(2,128)(2,1)S(1)} async-done(((bf16[256,2,320]{2,1,0:T(2,128)(2,1)}), bf16[256,2,320]{2,1,0:T(2,128)(2,1)S(1)}, u32[]{:S(2)}, u32[]{:S(2)}) %all-to-all-start) | async-done | bytes 327712 | tf_op jit(solution)/shard_map/all_to_all | solution.py:77
  39.1 0.8 reshape.216
  41.2 0.9 fusion.56
  42.1 0.9 fusion.36
  43.0 0.9 fusion.3
  43.8 0.9 fusion.2
  44.7 1.7 %fusion.25 = f32[3,256,256]{2,1,0:T(8,128)S(1)} fusion(f32[3,256,256]{1,2,0:T(8,128)S(1)} %fusion.3, f32[3,256,256]{1,2,0:T(8,128)S(1)} %fusion.2, f32[256,256]{0,1:T(8,128)S(1)} %copy.116, f32[256,256]{0,1:T(8,128)S(1)} %copy.115), kind=kOutput, calls=%fused_computation.54 | convolution fusion | flops 303497216 | bytes 2883584 | tf_op jit(solution)/shard_map/xkb,bl->xkl/dot_general | solution.py:14
  46.4 1.7 %fusion.27 = f32[3,256,256]{2,1,0:T(8,128)S(1)} fusion(f32[3,256,256]{1,2,0:T(8,128)S(1)} %fusion.2, f32[3,256,256]{1,2,0:T(8,128)S(1)} %fusion.3, f32[256,256]{0,1:T(8,128)S(1)} %copy.116, f32[256,256]{0,1:T(8,128)S(1)} %copy.115), kind=kOutput, calls=%fused_computation.56 | convolution fusion | flops 303497216 | bytes 2883584 | tf_op jit(solution)/shard_map/xkb,bl->xkl/dot_general | solution.py:14
  48.2 1.7 %fusion = f32[1,3,256,256]{3,2,1,0:T(8,128)S(1)} fusion(f32[3,256,256]{2,1,0:T(8,128)S(1)} %fusion.25, f32[3,256,256]{1,2,0:T(8,128)S(1)} %fusion.2, f32[3,256,256]{1,2,0:T(8,128)S(1)} %fusion.3, f32[256,256]{0,1:T(8,128)S(1)} %copy.116, f32[256,256]{0,1:T(8,128)S(1)} %copy.115), kind=kOutput, calls=%fused_computation.3 | convolution fusion | flops 303693824 | bytes 3670016 | tf_op jit(solution)/shard_map/xkb,bl->xkl/dot_general | solution.py:14
  49.9 1.7 %fusion.1 = f32[1,3,256,256]{3,2,1,0:T(8,128)S(1)} fusion(f32[3,256,256]{2,1,0:T(8,128)S(1)} %fusion.27, f32[3,256,256]{1,2,0:T(8,128)S(1)} %fusion.3, f32[3,256,256]{1,2,0:T(8,128)S(1)} %fusion.2, f32[256,256]{0,1:T(8,128)S(1)} %copy.116, f32[256,256]{0,1:T(8,128)S(1)} %copy.115), kind=kOutput, calls=%fused_computation.5 | convolution fusion | flops 303693824 | bytes 3670016 | tf_op jit(solution)/shard_map/xkb,bl->xkl/dot_general | solution.py:14
  51.9 1.7 %fusion.9 = f32[3,256,256]{1,2,0:T(8,128)S(1)} fusion(f32[1,1,256,256]{3,2,1,0:T(8,128)S(1)} %get-tuple-element.13, f32[1,1,256,256]{3,2,1,0:T(8,128)S(1)} %get-tuple-element.16, f32[1,1,256,256]{3,2,1,0:T(8,128)S(1)} %get-tuple-element.12), kind=kOutput, calls=%fused_computation.23 | convolution fusion | flops 303300608 | bytes 1572864 | tf_op jit(solution)/shard_map/xkl,lb->xkb/dot_general | solution.py:14
  53.6 1.5 %fusion.8 = f32[3,256,256]{1,2,0:T(8,128)S(1)} fusion(f32[1,1,256,256]{3,2,1,0:T(8,128)S(1)} %get-tuple-element.15, f32[1,1,256,256]{3,2,1,0:T(8,128)S(1)} %get-tuple-element.14, f32[1,1,256,256]{3,2,1,0:T(8,128)S(1)} %get-tuple-element.17), kind=kOutput, calls=%fused_computation.22 | convolution fusion | flops 303300608 | bytes 1572864 | tf_op jit(solution)/shard_map/xkl,lb->xkb/dot_general | solution.py:14
  55.1 1.5 %convolution_subtract_fusion = f32[3,256,256]{1,2,0:T(8,128)S(1)} fusion(f32[3,256,256]{1,2,0:T(8,128)S(1)} %fusion.9, f32[1,1,256,256]{3,2,1,0:T(8,128)S(1)} %get-tuple-element.15, f32[1,1,256,256]{3,2,1,0:T(8,128)S(1)} %get-tuple-element.14, f32[1,1,256,256]{3,2,1,0:T(8,128)S(1)} %get-tuple-element.17), kind=kOutput, calls=%fused_computation.1 | convolution fusion | flops 303497216 | bytes 2359296 | tf_op jit(solution)/shard_map/xkl,lb->xkb/dot_general | solution.py:14
  56.6 1.5 %convolution_add_fusion = f32[3,256,256]{1,2,0:T(8,128)S(1)} fusion(f32[3,256,256]{1,2,0:T(8,128)S(1)} %fusion.8, f32[1,1,256,256]{3,2,1,0:T(8,128)S(1)} %get-tuple-element.13, f32[1,1,256,256]{3,2,1,0:T(8,128)S(1)} %get-tuple-element.16, f32[1,1,256,256]{3,2,1,0:T(8,128)S(1)} %get-tuple-element.12), kind=kOutput, calls=%fused_computation | convolution fusion | flops 303497216 | bytes 2359296 | tf_op jit(solution)/shard_map/xkl,lb->xkb/dot_general | solution.py:14
  58.1 1.1 %fusion.49 = f32[3,256,128]{1,2,0:T(8,128)S(1)} fusion(f32[3,256,256]{1,2,0:T(8,128)S(1)} %convolution_subtract_fusion, f32[3,256,256]{1,2,0:T(8,128)S(1)} %convolution_add_fusion, f32[256,256]{0,1:T(8,128)S(1)} %copy.116, f32[256,256]{0,1:T(8,128)S(1)} %copy.115), kind=kOutput, calls=%fused_computation.97 | convolution fusion | flops 152043520 | bytes 2490368 | tf_op jit(solution)/shard_map/ak,xkb->xab/dot_general | solution.py:14
  59.2 1.1 %fusion.51 = f32[3,256,128]{1,2,0:T(8,128)S(1)} fusion(f32[3,256,256]{1,2,0:T(8,128)S(1)} %convolution_add_fusion, f32[3,256,256]{1,2,0:T(8,128)S(1)} %convolution_subtract_fusion, f32[256,256]{0,1:T(8,128)S(1)} %copy.116, f32[256,256]{0,1:T(8,128)S(1)} %copy.115), kind=kOutput, calls=%fused_computation.99 | convolution fusion | flops 152043520 | bytes 2490368 | tf_op jit(solution)/shard_map/ak,xkb->xab/dot_general | solution.py:14
  60.2 1.1 %fusion.5 = f32[1,3,128,256]{3,2,1,0:T(8,128)S(1)} fusion(f32[3,256,128]{1,2,0:T(8,128)S(1)} %fusion.49, f32[3,256,256]{1,2,0:T(8,128)S(1)} %convolution_add_fusion, f32[3,256,256]{1,2,0:T(8,128)S(1)} %convolution_subtract_fusion, f32[256,256]{0,1:T(8,128)S(1)} %copy.116, f32[256,256]{0,1:T(8,128)S(1)} %copy.115), kind=kOutput, calls=%fused_computation.12 | convolution fusion | flops 152240128 | bytes 2883584 | tf_op jit(solution)/shard_map/ak,xkb->xab/dot_general | solution.py:14
  61.3 1.1 %fusion.7 = f32[1,3,128,256]{3,2,1,0:T(8,128)S(1)} fusion(f32[3,256,128]{1,2,0:T(8,128)S(1)} %fusion.51, f32[3,256,256]{1,2,0:T(8,128)S(1)} %convolution_subtract_fusion, f32[3,256,256]{1,2,0:T(8,128)S(1)} %convolution_add_fusion, f32[256,256]{0,1:T(8,128)S(1)} %copy.116, f32[256,256]{0,1:T(8,128)S(1)} %copy.115), kind=kOutput, calls=%fused_computation.15 | convolution fusion | flops 152240128 | bytes 2883584 | tf_op jit(solution)/shard_map/ak,xkb->xab/dot_general | solution.py:14
  62.5 0.7 fusion.17
  63.2 0.7 fusion.18
  63.9 0.9 %reduce.1 = bf16[256,768]{1,0:T(8,128)(2,1)S(1)} reduce(bf16[256,1,768]{2,0,1:T(8,128)(2,1)S(1)} %pad_maximum_fusion, bf16[]{:T(256)} %broadcast.217), dimensions={1}, to_apply=%copy.129.reduce_sub_computation | reduce | bytes 786434 | tf_op jit(solution)/shard_map/concatenate | solution.py:121
  64.9 23.2 %all_to_all.10 = bf16[256,2,384]{2,1,0:T(2,128)(2,1)S(1)} all-to-all(bf16[256,2,384]{2,1,0:T(2,128)(2,1)S(1)} %reshape.217), channel_id=1, replica_groups=mesh['dp'=2,'seq'=128] {'dp','seq'}, dimensions={0} | all-to-all | bytes 786432 | tf_op jit(solution)/shard_map/all_to_all | solution.py:123
  88.4 0.7 copy.130
  89.3 0.8 fusion.43
  90.1 0.7 fusion.164
  (39 shorter events, 5.3 us)
Async XLA Ops:
  0.6 0.9 copy-start
  0.6 1.0 %copy-start.1 = (bf16[1,256,256]{2,1,0:T(8,128)(2,1)S(1)}, bf16[1,256,256]{2,1,0:T(8,128)(2,1)}, u32[]{:S(2)}) copy-start(bf16[1,256,256]{2,1,0:T(8,128)(2,1)} %param.9) | copy-start | bytes 393220
  1.6 1.0 %copy-start.3 = (bf16[1,256,256]{2,1,0:T(8,128)(2,1)S(1)}, bf16[1,256,256]{2,1,0:T(8,128)(2,1)}, u32[]{:S(2)}) copy-start(bf16[1,256,256]{2,1,0:T(8,128)(2,1)} %param.5) | copy-start | bytes 393220
  5.3 33.8 %all-to-all-start = ((bf16[256,2,320]{2,1,0:T(2,128)(2,1)}), bf16[256,2,320]{2,1,0:T(2,128)(2,1)S(1)}, u32[]{:S(2)}, u32[]{:S(2)}) async-start(bf16[256,2,320]{2,1,0:T(2,128)(2,1)} %reshape.215), calls=%async_computation | async-start | bytes 786432 | tf_op jit(solution)/shard_map/all_to_all | solution.py:77
  23.2 0.7 copy-start.4
  88.4 0.9 copy-start.2

commit v2 on v1

--- a/solution.py
+++ b/solution.py
@@ -22,38 +22,39 @@
     return (jnp.cos(phase), jnp.sin(phase))
 
 
-def spectra(x_re, x_im, outer, inner):
+def dft_tables(outer, inner):
     half = outer // 2
     padded = outer * inner
     k_idx = jnp.arange(outer, dtype=jnp.int32)
     a_idx = jnp.arange(half, dtype=jnp.int32)
     b_idx = jnp.arange(inner, dtype=jnp.int32)
     cos1, sin1 = angles(k_idx, a_idx, outer)
-    y_re = contract("ka,xab->xkb", cos1, x_re) + contract("ka,xab->xkb", sin1, x_im)
-    y_im = contract("ka,xab->xkb", cos1, x_im) - contract("ka,xab->xkb", sin1, x_re)
-    tw_re, tw_im = angles(k_idx, b_idx, padded)
-    y_re, y_im = (y_re * tw_re + y_im * tw_im, y_im * tw_re - y_re * tw_im)
+    first = jnp.stack(
+        [jnp.stack([cos1, sin1], axis=1), jnp.stack([-sin1, cos1], axis=1)], axis=1
+    )
     cos2, sin2 = angles(b_idx, b_idx, inner)
-    z_re = contract("xkb,bl->xkl", y_re, cos2) + contract("xkb,bl->xkl", y_im, sin2)
-    z_im = contract("xkb,bl->xkl", y_im, cos2) - contract("xkb,bl->xkl", y_re, sin2)
-    return z_re, z_im
+    second = jnp.stack(
+        [jnp.stack([cos2, -sin2], axis=1), jnp.stack([sin2, cos2], axis=1)], axis=0
+    )
+    twist = angles(k_idx, b_idx, padded)
+    return first, second, twist
 
 
-def timeline(z_re, z_im, outer, inner):
-    half = outer // 2
-    padded = outer * inner
-    k_idx = jnp.arange(outer, dtype=jnp.int32)
-    a_idx = jnp.arange(half, dtype=jnp.int32)
-    b_idx = jnp.arange(inner, dtype=jnp.int32)
-    cos2, sin2 = angles(b_idx, b_idx, inner)
-    u_re = contract("xkl,lb->xkb", z_re, cos2) - contract("xkl,lb->xkb", z_im, sin2)
-    u_im = contract("xkl,lb->xkb", z_im, cos2) + contract("xkl,lb->xkb", z_re, sin2)
-    tw_re, tw_im = angles(k_idx, b_idx, padded)
-    u_re, u_im = (u_re * tw_re - u_im * tw_im, u_im * tw_re + u_re * tw_im)
-    cos1, sin1 = angles(a_idx, k_idx, outer)
-    s_re = contract("ak,xkb->xab", cos1, u_re) - contract("ak,xkb->xab", sin1, u_im)
-    s_im = contract("ak,xkb->xab", cos1, u_im) + contract("ak,xkb->xab", sin1, u_re)
-    return s_re * (1.0 / padded), s_im * (1.0 / padded)
+def spectra(signal, tables):
+    first, second, (tw_re, tw_im) = tables
+    y = contract("ksra,xrab->xksb", first, signal)
+    y_re, y_im = y[:, :, 0], y[:, :, 1]
+    y = jnp.stack([y_re * tw_re + y_im * tw_im, y_im * tw_re - y_re * tw_im], axis=2)
+    return contract("xksb,sbtl->xktl", y, second)
+
+
+def timeline(spec, tables):
+    first, second, (tw_re, tw_im) = tables
+    padded = spec.shape[1] * spec.shape[3]
+    u = contract("xktl,ubtl->xkub", spec, second)
+    u_re, u_im = u[:, :, 0], u[:, :, 1]
+    u = jnp.stack([u_re * tw_re - u_im * tw_im, u_im * tw_re + u_re * tw_im], axis=2)
+    return contract("kuva,xkub->xvab", first, u) * (1.0 / padded)
 
 
 def on_device(values, gate_acts, filter_taps, skip_bias, grad_out):
@@ -85,31 +86,28 @@
     taps = owned(2 * rows, tap_rows).transpose(0, 2, 1, 3).reshape(per, 1, seq_count, rows)
 
     outer = 2 * seq_count
-    sig_re = jnp.stack([val[:, 0], grad_sig[:, 0], taps[:, 0]], axis=1).astype(jnp.float32)
-    sig_im = jnp.stack(
-        [val[:, 1], grad_sig[:, 1], jnp.zeros_like(taps[:, 0])], axis=1
+    tables = dft_tables(outer, rows)
+    signal = jnp.stack(
+        [
+            val,
+            grad_sig,
+            jnp.concatenate([taps, jnp.zeros_like(taps)], axis=1),
+        ],
+        axis=1,
     ).astype(jnp.float32)
-    z_re, z_im = spectra(
-        sig_re.reshape(per * 3, seq_count, rows), sig_im.reshape(per * 3, seq_count, rows), outer, rows
-    )
-    z_re = z_re.reshape(per, 3, outer, rows)
-    z_im = z_im.reshape(per, 3, outer, rows)
-    v_re, v_im = z_re[:, 0], z_im[:, 0]
-    g_re, g_im = z_re[:, 1], z_im[:, 1]
-    t_re, t_im = z_re[:, 2], z_im[:, 2]
-    conv_re = v_re * t_re - v_im * t_im
-    conv_im = v_re * t_im + v_im * t_re
-    corr_re = g_re * t_re + g_im * t_im
-    corr_im = g_im * t_re - g_re * t_im
-    filt_re = v_re * g_re + v_im * g_im
-    filt_im = v_re * g_im - v_im * g_re
-    prod_re = jnp.stack([conv_re, corr_re, filt_re], axis=1).reshape(per * 3, outer, rows)
-    prod_im = jnp.stack([conv_im, corr_im, filt_im], axis=1).reshape(per * 3, outer, rows)
-    out_re, out_im = timeline(prod_re, prod_im, outer, rows)
-    out_re = out_re.reshape(per, 3, seq_count, rows)
-    out_im = out_im.reshape(per, 3, seq_count, rows)
-    conv_part = jnp.stack([out_re[:, 0], out_im[:, 0]], axis=1)
-    back_part = jnp.stack([out_re[:, 1], out_im[:, 1]], axis=1)
+    spec = spectra(signal.reshape(per * 3, 2, seq_count, rows), tables)
+    spec = spec.reshape(per, 3, outer, 2, rows)
+    v_re, v_im = spec[:, 0, :, 0], spec[:, 0, :, 1]
+    g_re, g_im = spec[:, 1, :, 0], spec[:, 1, :, 1]
+    t_re, t_im = spec[:, 2, :, 0], spec[:, 2, :, 1]
+    conv = jnp.stack([v_re * t_re - v_im * t_im, v_re * t_im + v_im * t_re], axis=2)
+    corr = jnp.stack([g_re * t_re + g_im * t_im, g_im * t_re - g_re * t_im], axis=2)
+    filt = jnp.stack([v_re * g_re + v_im * g_im, v_re * g_im - v_im * g_re], axis=2)
+    prod = jnp.stack([conv, corr, filt], axis=1).reshape(per * 3, outer, 2, rows)
+    out = timeline(prod, tables).reshape(per, 3, 2, seq_count, rows)
+    conv_part = out[:, 0]
+    back_part = out[:, 1]
+    out_re = out[:, :, 0]
     total = dp_count * seq_count * rows
     grad_filter = (out_re[:, 2] * (1.0 / math.sqrt(total))).astype(jnp.bfloat16)
 

time: 91.7 us -> 76 us (0.83)
  matrix products: 20.8 us -> 4.45 us
  other arithmetic: 7.81 us -> 11.4 us
  local copies, waits for them, and re-layouts: 8.42 us -> 6.82 us
  waiting for transfers between devices: 14.6 us -> 13.3 us
    dot_general x16 -> x4, matrix products: 20.8 us -> 4.45 us  [contract(): jnp.einsum(pattern, left, right, precision=precise, preferred_element_typ...]
    sin x1 -> x3, other arithmetic: 0.97 us -> 2.6 us  [angles(): return (jnp.cos(phase), jnp.sin(phase))]
    unnamed x22 -> x16, local copies, waits for them, and re-layouts: 4.77 us -> 3.22 us
    neg x0 -> x2, other arithmetic: none -> 1.48 us  [the longest x1 0.98 us: dft_tables(): -sin2]
    all_to_all x1, waiting for transfers between devices: 14.6 us -> 13.3 us  [on_device(): got = lax.all_to_all(send, ALL, 0, 0, tiled=True)]
    cos x1 -> x0, other arithmetic: 0.96 us -> none  [angles(): return (jnp.cos(phase), jnp.sin(phase))]
    reshape x2, other arithmetic: 0.89 us -> 1.81 us  [on_device(): jnp.concatenate([values[0].T, gate_grad.T, taps_part.T], axis=1)]
  transfers between devices with their start and end apart: 1 -> 1, of which waited for: 1 -> 1; matrix products, arithmetic and copies ran while one was open for 3% -> 6% of each run, Pallas kernels for 0% -> 0%
where the time goes in v2:
time: 76 us; the launch traced here: 75.8 us
  blocking collectives  23.2 us (31%)
  starting transfers between devices  15.6 us (21%)
  waiting for transfers between devices  13.3 us (18%)
  other arithmetic  11.4 us (15%)
  local copies, waits for them, and re-layouts  6.82 us (9%)
  matrix products  4.45 us (6%)
  between operations  0.99 us (1%)
    all_to_all x1, blocking collectives, on_device(): lax.all_to_all(back, ALL, 0, 0, tiled=True).reshape(channels, 3, rows)  23.2 us
    all_to_all x1, starting transfers between devices, on_device(): got = lax.all_to_all(send, ALL, 0, 0, tiled=True)  15.6 us
    all_to_all x1, waiting for transfers between devices, on_device(): got = lax.all_to_all(send, ALL, 0, 0, tiled=True)  13.3 us
    dot_general x4, matrix products, contract(): jnp.einsum(pattern, left, right, precision=precise, preferred_element_typ...  4.45 us
    unnamed x16, local copies, waits for them, and re-layouts  3.22 us
    sin x3, other arithmetic, angles(): return (jnp.cos(phase), jnp.sin(phase))  2.6 us
    reshape x2, other arithmetic, on_device(): jnp.concatenate([values[0].T, gate_grad.T, taps_part.T], axis=1)  1.81 us
  transfers between devices with their start and end apart: 1, of which 1 were waited for; matrix products, arithmetic and copies ran while one was open for 6% of the time, Pallas kernels for 0%

profile of v2, /device:TPU:1, one launch (start us, length us, event | category | flops | bytes accessed | tf_op | source)
XLA Modules:
  0.0 75.8 jit_solution(963420389912193791)
XLA Ops:
  0.7 0.9 %copy-done = bf16[256,256]{1,0:T(8,128)(2,1)S(1)} copy-done((bf16[256,256]{1,0:T(8,128)(2,1)S(1)}, bf16[256,256]{1,0:T(8,128)(2,1)}, u32[]{:S(2)}) %copy-start) | copy-done | bytes 131096
  1.5 1.0 %fusion.52 = bf16[256,256]{0,1:T(8,128)(2,1)S(1)} fusion(bf16[1,256,256]{2,1,0:T(8,128)(2,1)} %param.9, bf16[1,256,256]{2,1,0:T(8,128)(2,1)} %param.6), kind=kLoop, calls=%fused_computation.87 | loop fusion | flops 262144 | bytes 393216 | tf_op jit(solution)/shard_map/transpose | solution.py:75
  2.5 0.9 %maximum_bitcast_fusion.18 = bf16[256,1,640]{0,2,1:T(8,128)(2,1)S(1)} fusion(bf16[256,128]{0,1:T(8,128)(2,1)S(1)} %dynamic-slice_bitcast_fusion, bf16[256,256]{0,1:T(8,128)(2,1)S(1)} %fusion.52, bf16[256,256]{0,1:T(8,128)(2,1)} %bitcast.178), kind=kLoop, calls=%fused_computation.51 | loop fusion | flops 983040 | bytes 655360 | tf_op jit(solution)/shard_map/reshape | solution.py:75
  3.5 0.5 broadcast.312
  4.0 0.9 %reduce = bf16[256,640]{0,1:T(8,128)(2,1)S(1)} reduce(bf16[256,1,640]{0,2,1:T(8,128)(2,1)S(1)} %maximum_bitcast_fusion.18, bf16[]{:T(256)} %broadcast.312), dimensions={1}, to_apply=%copy.72.reduce_sub_computation | reduce | bytes 655362 | tf_op jit(solution)/shard_map/reshape | solution.py:75
  4.9 0.2 copy.114
  5.1 1.1 %reshape.590 = bf16[256,2,320]{2,1,0:T(2,128)(2,1)} reshape(bf16[256,640]{1,0:T(8,128)(2,1)S(1)} %copy.114) | data formatting | bytes 655360
  6.2 15.6 %all-to-all-start = ((bf16[256,2,320]{2,1,0:T(2,128)(2,1)}), bf16[256,2,320]{2,1,0:T(2,128)(2,1)S(1)}, u32[]{:S(2)}, u32[]{:S(2)}) async-start(bf16[256,2,320]{2,1,0:T(2,128)(2,1)} %reshape.590), calls=%async_computation | async-start | bytes 786432 | tf_op jit(solution)/shard_map/all_to_all | solution.py:78
  21.8 1.0 %fusion.62 = f32[256,1,256]{2,0,1:T(8,128)S(1)} fusion(), kind=kLoop, calls=%fused_computation.102 | loop fusion | flops 983040 | bytes 262144 | tf_op jit(solution)/shard_map/neg | solution.py:37
  22.8 0.5 fusion.66
  23.3 0.6 dynamic_slice.10
  23.9 0.5 fusion.64
  24.4 1.0 %fusion.57 = (f32[256,256]{0,1:T(8,128)S(1)}, f32[256,256]{0,1:T(8,128)S(1)}) fusion(), kind=kLoop, calls=%fused_computation.96 | loop fusion | flops 917504 | bytes 524288 | tf_op jit(solution)/shard_map/sin | solution.py:22
  25.5 1.0 %fusion.55 = (f32[256,1,256]{2,0,1:T(8,128)S(1)}, f32[256,1,256]{2,0,1:T(8,128)S(1)}) fusion(), kind=kLoop, calls=%fused_computation.94 | loop fusion | flops 917504 | bytes 524288 | tf_op jit(solution)/shard_map/sin | solution.py:22
  26.7 13.3 %all-to-all-done = bf16[256,2,320]{2,1,0:T(2,128)(2,1)S(1)} async-done(((bf16[256,2,320]{2,1,0:T(2,128)(2,1)}), bf16[256,2,320]{2,1,0:T(2,128)(2,1)S(1)}, u32[]{:S(2)}, u32[]{:S(2)}) %all-to-all-start) | async-done | bytes 327712 | tf_op jit(solution)/shard_map/all_to_all | solution.py:78
  39.9 0.6 reshape.591
  40.7 0.5 fusion.73
  41.7 0.6 convolution_bitcast_fusion
  42.3 0.2 multiply_add_fusion.1
  42.5 1.5 %fusion.14 = f32[1,3,256,2,256]{4,2,3,1,0:T(8,128)S(1)} fusion(f32[3,256,1,256]{1,3,2,0:T(8,128)S(1)} %get-tuple-element.15, f32[3,256,1,256]{1,3,2,0:T(8,128)S(1)} %get-tuple-element.14, f32[1,256,2,256]{3,1,0,2:T(8,128)S(1)} %get-tuple-element.31, f32[1,256,2,256]{3,1,0,2:T(8,128)S(1)} %get-tuple-element.30), kind=kOutput, calls=%fused_computation.16 | convolution fusion | flops 1208614912 | bytes 4194304 | tf_op jit(solution)/shard_map/xksb,sbtl->xktl/dot_general | solution.py:14
  44.3 1.5 %fusion.13 = f32[3,256,2,256]{1,3,2,0:T(8,128)S(1)} fusion(f32[1,1,256,2,256]{4,2,3,1,0:T(8,128)S(1)} %maximum_bitcast_fusion.13, f32[1,1,256,2,256]{4,2,3,1,0:T(8,128)S(1)} %maximum_bitcast_fusion.12, f32[1,1,256,2,256]{4,2,3,1,0:T(8,128)S(1)} %maximum_bitcast_fusion.11, f32[1,256,2,256]{3,1,0,2:T(8,128)S(1)} %get-tuple-element.31, ...), kind=kOutput, calls=%fused_computation.15 | convolution fusion | flops 1209008128 | bytes 4194304 | tf_op jit(solution)/shard_map/xktl,ubtl->xkub/dot_general | solution.py:14
  45.8 0.2 multiply_subtract_fusion
  46.0 0.9 %fusion.21 = f32[1,3,2,128,256]{4,3,2,1,0:T(8,128)S(1)} fusion(f32[3,256,1,256]{1,3,2,0:T(8,128)S(1)} %get-tuple-element.13, f32[3,256,1,256]{1,3,2,0:T(8,128)S(1)} %get-tuple-element.12, f32[256,1,2,128]{3,0,2,1:T(8,128)S(1)} %get-tuple-element.33, f32[256,1,2,128]{3,0,2,1:T(8,128)S(1)} %get-tuple-element.32), kind=kOutput, calls=%fused_computation.20 | convolution fusion | flops 604700672 | bytes 2883584 | tf_op jit(solution)/shard_map/kuva,xkub->xvab/dot_general | solution.py:14
  47.0 0.7 fusion.40
  47.7 0.7 fusion.41
  48.4 0.9 %reduce.1 = bf16[256,768]{1,0:T(8,128)(2,1)S(1)} reduce(bf16[256,1,768]{2,0,1:T(8,128)(2,1)S(1)} %pad_maximum_fusion.1, bf16[]{:T(256)} %broadcast.312), dimensions={1}, to_apply=%copy.86.reduce_sub_computation | reduce | bytes 786434 | tf_op jit(solution)/shard_map/concatenate | solution.py:119
  49.5 23.2 %all_to_all.10 = bf16[256,2,384]{2,1,0:T(2,128)(2,1)S(1)} all-to-all(bf16[256,2,384]{2,1,0:T(2,128)(2,1)S(1)} %reshape.592), channel_id=1, replica_groups=mesh['dp'=2,'seq'=128] {'dp','seq'}, dimensions={0} | all-to-all | bytes 786432 | tf_op jit(solution)/shard_map/all_to_all | solution.py:121
  72.6 0.3 reshape.593
  72.9 0.7 copy.87
  73.7 0.8 fusion.51
  74.4 0.7 fusion.74
  75.1 0.7 convert_bitcast_fusion.1
  (29 shorter events, 1.2 us)
Async XLA Ops:
  0.6 0.9 %copy-start = (bf16[256,256]{1,0:T(8,128)(2,1)S(1)}, bf16[256,256]{1,0:T(8,128)(2,1)}, u32[]{:S(2)}) copy-start(bf16[256,256]{1,0:T(8,128)(2,1)} %param.7) | copy-start | bytes 393220
  4.0 19.3 %copy-start.3 = (f32[256]{0:T(256)S(1)}, f32[256]{0:T(256)}, u32[]{:S(2)}) copy-start(f32[256]{0:T(256)} %param.8) | copy-start | bytes 3076
  6.2 33.8 %all-to-all-start = ((bf16[256,2,320]{2,1,0:T(2,128)(2,1)}), bf16[256,2,320]{2,1,0:T(2,128)(2,1)S(1)}, u32[]{:S(2)}, u32[]{:S(2)}) async-start(bf16[256,2,320]{2,1,0:T(2,128)(2,1)} %reshape.590), calls=%async_computation | async-start | bytes 786432 | tf_op jit(solution)/shard_map/all_to_all | solution.py:78
  49.4 24.2 %copy-start.1 = (bf16[1,256,256]{2,1,0:T(8,128)(2,1)S(1)}, bf16[1,256,256]{2,1,0:T(8,128)(2,1)}, u32[]{:S(2)}) copy-start(bf16[1,256,256]{2,1,0:T(8,128)(2,1)} %param.9) | copy-start | bytes 393220
  49.4 24.2 %copy-start.2 = (bf16[1,256,256]{2,1,0:T(8,128)(2,1)S(1)}, bf16[1,256,256]{2,1,0:T(8,128)(2,1)}, u32[]{:S(2)}) copy-start(bf16[1,256,256]{2,1,0:T(8,128)(2,1)} %param.6) | copy-start | bytes 393220

commit v3 on v2

--- a/solution.py
+++ b/solution.py
@@ -72,10 +72,10 @@
     gate_grad = (grad_out[0].astype(jnp.float32) * gate_acts[0].astype(jnp.float32)).astype(
         jnp.bfloat16
     )
-    send = jnp.concatenate([values[0].T, gate_grad.T, taps_part.T], axis=1).reshape(
-        dev_count, per, 2 * rows + tap_rows
-    )
-    got = lax.all_to_all(send, ALL, 0, 0, tiled=True)
+    width = 2 * rows + tap_rows
+    send = jnp.concatenate([values[0], gate_grad, taps_part], axis=0).T
+    send = send.reshape(dev_count, 2, per * width // 2)
+    got = lax.all_to_all(send, ALL, 0, 0, tiled=True).reshape(dev_count, per, width)
 
     def owned(lo, width):
         part = got[:, :, lo : lo + width].reshape(dp_count, seq_count, per, width)
@@ -117,7 +117,7 @@
 
     filt_rep = jnp.broadcast_to(grad_filter[:, None], (per, dp_count, seq_count, rows))
     back = jnp.concatenate([hyena_pre, grad_values, filt_rep], axis=3)
-    back = back.transpose(1, 2, 0, 3).reshape(dev_count, per, 3 * rows)
+    back = back.transpose(1, 2, 0, 3).reshape(dev_count, 2, per * 3 * rows // 2)
     back = lax.all_to_all(back, ALL, 0, 0, tiled=True).reshape(channels, 3, rows)
     hyena_pre = back[:, 0].T.astype(jnp.float32)
     grad_values = back[:, 1].T[None]

time: 76 us -> 72.4 us (0.953)
  other arithmetic: 11.4 us -> 8.99 us
  local copies, waits for them, and re-layouts: 6.82 us -> 5.75 us
    unnamed x16 -> x8, local copies, waits for them, and re-layouts: 3.22 us -> 0.9 us
    reshape x2 -> x0, other arithmetic: 1.81 us -> none  [on_device(): jnp.concatenate([values[0].T, gate_grad.T, taps_part.T], axis=1)]
    transpose x1 -> x0, other arithmetic: 1 us -> none  [on_device(): send = jnp.concatenate([values[0].T, gate_grad.T, taps_part.T], axis=1).r...]
    concatenate x0 -> x1, other arithmetic: none -> 0.93 us  [on_device(): send = jnp.concatenate([values[0], gate_grad, taps_part], axis=0).T]
    concatenate x2 -> x1, other arithmetic: 0.95 us -> 0.03 us  [on_device(): back = jnp.concatenate([hyena_pre, grad_values, filt_rep], axis=3)]
  transfers between devices with their start and end apart: 1 -> 1, of which waited for: 1 -> 1; matrix products, arithmetic and copies ran while one was open for 6% -> 7% of each run, Pallas kernels for 0% -> 0%
where the time goes in v3:
time: 72.4 us; the launch traced here: 72.2 us
  blocking collectives  23.2 us (32%)
  starting transfers between devices  15.6 us (22%)
  waiting for transfers between devices  13.3 us (18%)
  other arithmetic  8.99 us (12%)
  local copies, waits for them, and re-layouts  5.75 us (8%)
  matrix products  4.33 us (6%)
  between operations  0.99 us (1%)
    all_to_all x1, blocking collectives, on_device(): lax.all_to_all(back, ALL, 0, 0, tiled=True).reshape(channels, 3, rows)  23.2 us
    all_to_all x1, starting transfers between devices, on_device(): lax.all_to_all(send, ALL, 0, 0, tiled=True).reshape(dev_count, per, width)  15.6 us
    all_to_all x1, waiting for transfers between devices, on_device(): lax.all_to_all(send, ALL, 0, 0, tiled=True).reshape(dev_count, per, width)  13.3 us
    dot_general x4, matrix products, contract(): jnp.einsum(pattern, left, right, precision=precise, preferred_element_typ...  4.33 us
    sin x3, other arithmetic, angles(): return (jnp.cos(phase), jnp.sin(phase))  2.6 us
  transfers between devices with their start and end apart: 1, of which 1 were waited for; matrix products, arithmetic and copies ran while one was open for 7% of the time, Pallas kernels for 0%

profile of v3, /device:TPU:1, one launch (start us, length us, event | category | flops | bytes accessed | tf_op | source)
XLA Modules:
  0.0 72.2 jit_solution(6358461687360895108)
XLA Ops:
  0.7 0.9 %copy-done = bf16[256,256]{1,0:T(8,128)(2,1)S(1)} copy-done((bf16[256,256]{1,0:T(8,128)(2,1)S(1)}, bf16[256,256]{1,0:T(8,128)(2,1)}, u32[]{:S(2)}) %copy-start) | copy-done | bytes 131096
  1.5 1.0 %fusion.27 = bf16[256,256]{1,0:T(8,128)(2,1)S(1)} fusion(bf16[1,256,256]{2,1,0:T(8,128)(2,1)} %param.9, bf16[1,256,256]{2,1,0:T(8,128)(2,1)} %param.6), kind=kLoop, calls=%fused_computation.55 | loop fusion | flops 262144 | bytes 393216 | tf_op jit(solution)/shard_map/convert_element_type | solution.py:72
  2.5 0.9 %pad_maximum_fusion.3 = bf16[640,256]{1,0:T(8,128)(2,1)S(1)} fusion(bf16[128,256]{1,0:T(8,128)(2,1)S(1)} %constant_dynamic-slice_fusion, bf16[256,256]{1,0:T(8,128)(2,1)S(1)} %fusion.27, bf16[256,256]{1,0:T(8,128)(2,1)} %bitcast.183), kind=kLoop, calls=%fused_computation.53 | loop fusion | flops 983040 | bytes 655360 | tf_op jit(solution)/shard_map/concatenate | solution.py:76
  3.5 1.1 %copy.49 = bf16[256,2,320]{2,1,0:T(2,128)(2,1)} copy(bf16[256,2,320]{0,2,1:T(8,128)(2,1)S(1)} %bitcast.176) | data formatting | bytes 655360 | tf_op jit(solution)/shard_map/reshape | solution.py:77
  4.6 15.6 %all-to-all-start = ((bf16[256,2,320]{2,1,0:T(2,128)(2,1)}), bf16[256,2,320]{2,1,0:T(2,128)(2,1)S(1)}, u32[]{:S(2)}, u32[]{:S(2)}) async-start(bf16[256,2,320]{2,1,0:T(2,128)(2,1)} %copy.49), calls=%async_computation | async-start | bytes 786432 | tf_op jit(solution)/shard_map/all_to_all | solution.py:78
  20.2 0.5 fusion.60
  20.8 0.5 fusion.62
  21.3 0.6 dynamic_slice.10
  21.9 1.0 %fusion.58 = f32[256,1,256]{2,0,1:T(8,128)S(1)} fusion(), kind=kLoop, calls=%fused_computation.107 | loop fusion | flops 983040 | bytes 262144 | tf_op jit(solution)/shard_map/neg | solution.py:37
  22.9 1.0 %fusion.53 = (f32[256,256]{0,1:T(8,128)S(1)}, f32[256,256]{0,1:T(8,128)S(1)}) fusion(), kind=kLoop, calls=%fused_computation.101 | loop fusion | flops 917504 | bytes 524288 | tf_op jit(solution)/shard_map/sin | solution.py:22
  23.9 1.0 %fusion.51 = (f32[256,1,256]{2,0,1:T(8,128)S(1)}, f32[256,1,256]{2,0,1:T(8,128)S(1)}) fusion(), kind=kLoop, calls=%fused_computation.99 | loop fusion | flops 917504 | bytes 524288 | tf_op jit(solution)/shard_map/sin | solution.py:22
  25.1 13.3 %all-to-all-done = bf16[256,2,320]{2,1,0:T(2,128)(2,1)S(1)} async-done(((bf16[256,2,320]{2,1,0:T(2,128)(2,1)}), bf16[256,2,320]{2,1,0:T(2,128)(2,1)S(1)}, u32[]{:S(2)}, u32[]{:S(2)}) %all-to-all-start) | async-done | bytes 327712 | tf_op jit(solution)/shard_map/all_to_all | solution.py:78
  38.3 0.5 copy.50
  39.0 0.1 copy.55
  39.5 0.1 copy.54
  39.6 0.6 convolution_bitcast_fusion
  40.2 0.2 multiply_add_fusion.1
  40.4 1.5 %fusion.12 = f32[1,3,256,2,256]{4,2,3,1,0:T(8,128)S(1)} fusion(f32[3,256,1,256]{1,3,2,0:T(8,128)S(1)} %get-tuple-element.7, f32[3,256,1,256]{1,3,2,0:T(8,128)S(1)} %get-tuple-element.6, f32[1,256,2,256]{3,1,0,2:T(8,128)S(1)} %get-tuple-element.25, f32[1,256,2,256]{3,1,0,2:T(8,128)S(1)} %get-tuple-element.24), kind=kOutput, calls=%fused_computation.15 | convolution fusion | flops 1208614912 | bytes 4194304 | tf_op jit(solution)/shard_map/xksb,sbtl->xktl/dot_general | solution.py:14
  42.2 1.5 %fusion.11 = f32[3,256,2,256]{1,3,2,0:T(8,128)S(1)} fusion(f32[1,1,256,2,256]{4,2,3,1,0:T(8,128)S(1)} %maximum_bitcast_fusion.20, f32[1,1,256,2,256]{4,2,3,1,0:T(8,128)S(1)} %maximum_bitcast_fusion.19, f32[1,1,256,2,256]{4,2,3,1,0:T(8,128)S(1)} %maximum_bitcast_fusion.18, f32[1,256,2,256]{3,1,0,2:T(8,128)S(1)} %get-tuple-element.25, ...), kind=kOutput, calls=%fused_computation.14 | convolution fusion | flops 1209008128 | bytes 4194304 | tf_op jit(solution)/shard_map/xktl,ubtl->xkub/dot_general | solution.py:14
  43.7 0.2 multiply_subtract_fusion
  43.9 0.7 convert_multiply_fusion.4
  44.6 0.1 copy.63
  44.7 0.1 copy.64
  44.8 0.1 copy.65
  45.0 0.1 copy.66
  45.1 0.8 %fusion.15 = f32[1,3,2,128,256]{3,4,2,1,0:T(8,128)S(1)} fusion(f32[3,256,1,256]{1,3,2,0:T(8,128)S(1)} %get-tuple-element.5, f32[3,256,1,256]{1,3,2,0:T(8,128)S(1)} %get-tuple-element.4, f32[256,1,2,128]{3,0,2,1:T(8,128)S(1)} %get-tuple-element.27, f32[256,1,2,128]{3,0,2,1:T(8,128)S(1)} %get-tuple-element.26), kind=kOutput, calls=%fused_computation.19 | convolution fusion | flops 604700672 | bytes 2883584 | tf_op jit(solution)/shard_map/kuva,xkub->xvab/dot_general | solution.py:14
  46.1 0.2 copy.67
  46.4 23.2 %all_to_all.10 = bf16[256,2,384]{2,1,0:T(2,128)(2,1)S(1)} all-to-all(bf16[256,2,384]{2,1,0:T(2,128)(2,1)S(1)} %reshape_transpose.3), channel_id=1, replica_groups=mesh['dp'=2,'seq'=128] {'dp','seq'}, dimensions={0} | all-to-all | bytes 786432 | tf_op jit(solution)/shard_map/all_to_all | solution.py:121
  69.6 0.5 copy.68
  70.1 0.7 fusion.67
  70.7 0.8 %fusion.48 = (bf16[1,256,256]{2,1,0:T(8,128)(2,1)}, bf16[1,256,256]{2,1,0:T(8,128)(2,1)}) fusion(bf16[1,256,256]{2,1,0:T(8,128)(2,1)S(1)} %copy-done.1, bf16[256,3,256]{0,2,1:T(8,128)(2,1)S(1)} %bitcast.175, bf16[1,256,256]{2,1,0:T(8,128)(2,1)S(1)} %copy-done.2), kind=kLoop, calls=%fused_computation.92 | loop fusion | flops 458752 | bytes 655360 | tf_op jit(solution)/shard_map/broadcast_in_dim | solution.py:128
  71.5 0.7 convert_bitcast_fusion.1
  (28 shorter events, 1.1 us)
Async XLA Ops:
  0.6 0.9 %copy-start = (bf16[256,256]{1,0:T(8,128)(2,1)S(1)}, bf16[256,256]{1,0:T(8,128)(2,1)}, u32[]{:S(2)}) copy-start(bf16[256,256]{1,0:T(8,128)(2,1)} %param.7) | copy-start | bytes 393220
  0.6 20.6 %copy-start.3 = (f32[256]{0:T(256)S(1)}, f32[256]{0:T(256)}, u32[]{:S(2)}) copy-start(f32[256]{0:T(256)} %param.8) | copy-start | bytes 3076
  4.6 33.8 %all-to-all-start = ((bf16[256,2,320]{2,1,0:T(2,128)(2,1)}), bf16[256,2,320]{2,1,0:T(2,128)(2,1)S(1)}, u32[]{:S(2)}, u32[]{:S(2)}) async-start(bf16[256,2,320]{2,1,0:T(2,128)(2,1)} %copy.49), calls=%async_computation | async-start | bytes 786432 | tf_op jit(solution)/shard_map/all_to_all | solution.py:78
  46.3 24.5 %copy-start.1 = (bf16[1,256,256]{2,1,0:T(8,128)(2,1)S(1)}, bf16[1,256,256]{2,1,0:T(8,128)(2,1)}, u32[]{:S(2)}) copy-start(bf16[1,256,256]{2,1,0:T(8,128)(2,1)} %param.9) | copy-start | bytes 393220
  46.3 24.5 %copy-start.2 = (bf16[1,256,256]{2,1,0:T(8,128)(2,1)S(1)}, bf16[1,256,256]{2,1,0:T(8,128)(2,1)}, u32[]{:S(2)}) copy-start(bf16[1,256,256]{2,1,0:T(8,128)(2,1)} %param.6) | copy-start | bytes 393220

commit v4 on v3

--- a/solution.py
+++ b/solution.py
@@ -73,9 +73,11 @@
         jnp.bfloat16
     )
     width = 2 * rows + tap_rows
-    send = jnp.concatenate([values[0], gate_grad, taps_part], axis=0).T
-    send = send.reshape(dev_count, 2, per * width // 2)
-    got = lax.all_to_all(send, ALL, 0, 0, tiled=True).reshape(dev_count, per, width)
+    spare = (-per * width) % 256
+    pad = jnp.zeros((spare // per, channels), values.dtype)
+    send = jnp.concatenate([values[0], gate_grad, taps_part, pad], axis=0).T
+    send = send.reshape(dev_count, 2, (per * width + spare) // 2)
+    got = lax.all_to_all(send, ALL, 0, 0, tiled=True).reshape(dev_count, per, -1)
 
     def owned(lo, width):
         part = got[:, :, lo : lo + width].reshape(dp_count, seq_count, per, width)

time: 72.4 us -> 71.7 us (level)
  local copies, waits for them, and re-layouts: 5.75 us -> 4.97 us
where the time goes in v4:
time: 71.7 us; the launch traced here: 71.5 us
  blocking collectives  23.2 us (32%)
  starting transfers between devices  15.6 us (22%)
  waiting for transfers between devices  13.3 us (19%)
  other arithmetic  9.13 us (13%)
  local copies, waits for them, and re-layouts  4.97 us (7%)
  matrix products  4.33 us (6%)
  between operations  0.96 us (1%)
    all_to_all x1, blocking collectives, on_device(): lax.all_to_all(back, ALL, 0, 0, tiled=True).reshape(channels, 3, rows)  23.2 us
    all_to_all x1, starting transfers between devices, on_device(): lax.all_to_all(send, ALL, 0, 0, tiled=True).reshape(dev_count, per, -1)  15.6 us
    all_to_all x1, waiting for transfers between devices, on_device(): lax.all_to_all(send, ALL, 0, 0, tiled=True).reshape(dev_count, per, -1)  13.3 us
    dot_general x4, matrix products, contract(): jnp.einsum(pattern, left, right, precision=precise, preferred_element_typ...  4.33 us
    sin x3, other arithmetic, angles(): return (jnp.cos(phase), jnp.sin(phase))  2.6 us
  transfers between devices with their start and end apart: 1, of which 1 were waited for; matrix products, arithmetic and copies ran while one was open for 7% of the time, Pallas kernels for 0%

profile of v4, /device:TPU:1, one launch (start us, length us, event | category | flops | bytes accessed | tf_op | source)
XLA Modules:
  0.0 71.5 jit_solution(11805843350108820017)
XLA Ops:
  0.7 0.9 %copy-done = bf16[256,256]{1,0:T(8,128)(2,1)S(1)} copy-done((bf16[256,256]{1,0:T(8,128)(2,1)S(1)}, bf16[256,256]{1,0:T(8,128)(2,1)}, u32[]{:S(2)}) %copy-start) | copy-done | bytes 131096
  1.5 1.0 %fusion.27 = bf16[256,256]{1,0:T(8,128)(2,1)S(1)} fusion(bf16[1,256,256]{2,1,0:T(8,128)(2,1)} %param.9, bf16[1,256,256]{2,1,0:T(8,128)(2,1)} %param.6), kind=kLoop, calls=%fused_computation.55 | loop fusion | flops 262144 | bytes 393216 | tf_op jit(solution)/shard_map/convert_element_type | solution.py:72
  2.6 1.1 %maximum_maximum_fusion = bf16[768,256]{1,0:T(8,128)(2,1)S(1)} fusion(bf16[128,256]{1,0:T(8,128)(2,1)S(1)} %constant_dynamic-slice_fusion, bf16[256,256]{1,0:T(8,128)(2,1)S(1)} %fusion.27, bf16[256,256]{1,0:T(8,128)(2,1)} %bitcast.179, bf16[768]{0:T(1024)(128)(2,1)S(1)} %pad.35.clone), kind=kLoop, calls=%fused_computation.38 | loop fusion | flops 1572864 | bytes 722432 | tf_op jit(solution)/shard_map/concatenate | solution.py:78
  3.7 1.1 %copy.31 = bf16[256,2,384]{2,1,0:T(2,128)(2,1)} copy(bf16[256,2,384]{0,2,1:T(8,128)(2,1)S(1)} %bitcast.172) | data formatting | bytes 786432 | tf_op jit(solution)/shard_map/reshape | solution.py:79
  4.8 15.6 %all-to-all-start = ((bf16[256,2,384]{2,1,0:T(2,128)(2,1)}), bf16[256,2,384]{2,1,0:T(2,128)(2,1)S(1)}, u32[]{:S(2)}, u32[]{:S(2)}) async-start(bf16[256,2,384]{2,1,0:T(2,128)(2,1)} %copy.31), calls=%async_computation | async-start | bytes 786432 | tf_op jit(solution)/shard_map/all_to_all | solution.py:80
  20.4 0.5 fusion.62
  20.9 0.6 dynamic_slice.10
  21.5 0.5 fusion.60
  22.1 1.0 %fusion.58 = f32[256,1,256]{2,0,1:T(8,128)S(1)} fusion(), kind=kLoop, calls=%fused_computation.107 | loop fusion | flops 983040 | bytes 262144 | tf_op jit(solution)/shard_map/neg | solution.py:37
  23.0 1.0 %fusion.53 = (f32[256,256]{0,1:T(8,128)S(1)}, f32[256,256]{0,1:T(8,128)S(1)}) fusion(), kind=kLoop, calls=%fused_computation.101 | loop fusion | flops 917504 | bytes 524288 | tf_op jit(solution)/shard_map/sin | solution.py:22
  24.1 1.0 %fusion.51 = (f32[256,1,256]{2,0,1:T(8,128)S(1)}, f32[256,1,256]{2,0,1:T(8,128)S(1)}) fusion(), kind=kLoop, calls=%fused_computation.99 | loop fusion | flops 917504 | bytes 524288 | tf_op jit(solution)/shard_map/sin | solution.py:22
  25.2 13.3 %all-to-all-done = bf16[256,2,384]{2,1,0:T(2,128)(2,1)S(1)} async-done(((bf16[256,2,384]{2,1,0:T(2,128)(2,1)}), bf16[256,2,384]{2,1,0:T(2,128)(2,1)S(1)}, u32[]{:S(2)}, u32[]{:S(2)}) %all-to-all-start) | async-done | bytes 393248 | tf_op jit(solution)/shard_map/all_to_all | solution.py:80
  38.5 0.2 reshape.616
  38.8 0.1 copy.33
  38.9 0.1 copy.34
  39.1 0.1 copy.32
  39.2 0.6 convolution_bitcast_fusion
  39.8 0.2 multiply_add_fusion.1
  40.0 1.5 %fusion.12 = f32[1,3,256,2,256]{4,2,3,1,0:T(8,128)S(1)} fusion(f32[3,256,1,256]{1,3,2,0:T(8,128)S(1)} %get-tuple-element.7, f32[3,256,1,256]{1,3,2,0:T(8,128)S(1)} %get-tuple-element.6, f32[1,256,2,256]{3,1,0,2:T(8,128)S(1)} %get-tuple-element.25, f32[1,256,2,256]{3,1,0,2:T(8,128)S(1)} %get-tuple-element.24), kind=kOutput, calls=%fused_computation.15 | convolution fusion | flops 1208614912 | bytes 4194304 | tf_op jit(solution)/shard_map/xksb,sbtl->xktl/dot_general | solution.py:14
  41.5 0.1 subtract_bitcast_fusion.2
  41.8 1.5 %fusion.11 = f32[3,256,2,256]{1,3,2,0:T(8,128)S(1)} fusion(f32[1,1,256,2,256]{4,2,3,1,0:T(8,128)S(1)} %maximum_bitcast_fusion.20, f32[1,1,256,2,256]{4,2,3,1,0:T(8,128)S(1)} %maximum_bitcast_fusion.19, f32[1,1,256,2,256]{4,2,3,1,0:T(8,128)S(1)} %maximum_bitcast_fusion.18, f32[1,256,2,256]{3,1,0,2:T(8,128)S(1)} %get-tuple-element.25, ...), kind=kOutput, calls=%fused_computation.14 | convolution fusion | flops 1209008128 | bytes 4194304 | tf_op jit(solution)/shard_map/xktl,ubtl->xkub/dot_general | solution.py:14
  43.3 0.2 multiply_subtract_fusion
  43.5 0.7 convert_multiply_fusion.4
  44.2 0.1 copy.41
  44.3 0.1 copy.42
  44.4 0.8 %fusion.15 = f32[1,3,2,128,256]{3,4,2,1,0:T(8,128)S(1)} fusion(f32[3,256,1,256]{1,3,2,0:T(8,128)S(1)} %get-tuple-element.5, f32[3,256,1,256]{1,3,2,0:T(8,128)S(1)} %get-tuple-element.4, f32[256,1,2,128]{3,0,2,1:T(8,128)S(1)} %get-tuple-element.27, f32[256,1,2,128]{3,0,2,1:T(8,128)S(1)} %get-tuple-element.26), kind=kOutput, calls=%fused_computation.19 | convolution fusion | flops 604700672 | bytes 2883584 | tf_op jit(solution)/shard_map/kuva,xkub->xvab/dot_general | solution.py:14
  45.4 0.2 copy.43
  45.7 23.2 %all_to_all.10 = bf16[256,2,384]{2,1,0:T(2,128)(2,1)S(1)} all-to-all(bf16[256,2,384]{2,1,0:T(2,128)(2,1)S(1)} %reshape_transpose.3), channel_id=1, replica_groups=mesh['dp'=2,'seq'=128] {'dp','seq'}, dimensions={0} | all-to-all | bytes 786432 | tf_op jit(solution)/shard_map/all_to_all | solution.py:123
  68.9 0.5 copy.44
  69.4 0.7 fusion.67
  70.1 0.8 %fusion.48 = (bf16[1,256,256]{2,1,0:T(8,128)(2,1)}, bf16[1,256,256]{2,1,0:T(8,128)(2,1)}) fusion(bf16[1,256,256]{2,1,0:T(8,128)(2,1)S(1)} %copy-done.1, bf16[256,3,256]{0,2,1:T(8,128)(2,1)S(1)} %bitcast.171, bf16[1,256,256]{2,1,0:T(8,128)(2,1)S(1)} %copy-done.2), kind=kLoop, calls=%fused_computation.92 | loop fusion | flops 458752 | bytes 655360 | tf_op jit(solution)/shard_map/broadcast_in_dim | solution.py:130
  70.8 0.7 convert_bitcast_fusion.1
  (25 shorter events, 0.6 us)
Async XLA Ops:
  0.6 0.9 %copy-start = (bf16[256,256]{1,0:T(8,128)(2,1)S(1)}, bf16[256,256]{1,0:T(8,128)(2,1)}, u32[]{:S(2)}) copy-start(bf16[256,256]{1,0:T(8,128)(2,1)} %param.7) | copy-start | bytes 393220
  0.6 20.3 %copy-start.3 = (f32[256]{0:T(256)S(1)}, f32[256]{0:T(256)}, u32[]{:S(2)}) copy-start(f32[256]{0:T(256)} %param.8) | copy-start | bytes 3076
  4.8 33.8 %all-to-all-start = ((bf16[256,2,384]{2,1,0:T(2,128)(2,1)}), bf16[256,2,384]{2,1,0:T(2,128)(2,1)S(1)}, u32[]{:S(2)}, u32[]{:S(2)}) async-start(bf16[256,2,384]{2,1,0:T(2,128)(2,1)} %copy.31), calls=%async_computation | async-start | bytes 786432 | tf_op jit(solution)/shard_map/all_to_all | solution.py:80
  45.6 24.5 %copy-start.1 = (bf16[1,256,256]{2,1,0:T(8,128)(2,1)S(1)}, bf16[1,256,256]{2,1,0:T(8,128)(2,1)}, u32[]{:S(2)}) copy-start(bf16[1,256,256]{2,1,0:T(8,128)(2,1)} %param.9) | copy-start | bytes 393220
  45.6 24.5 %copy-start.2 = (bf16[1,256,256]{2,1,0:T(8,128)(2,1)S(1)}, bf16[1,256,256]{2,1,0:T(8,128)(2,1)}, u32[]{:S(2)}) copy-start(bf16[1,256,256]{2,1,0:T(8,128)(2,1)} %param.6) | copy-start | bytes 393220
